TPU v7x, 256 devices: a whole 4x4x8 slice. The times are simulated.
256 devices in a mesh: head: 8 (over y, core), ctx: 32 (over z, x).
Axes of the slice: x: 4, y: 4, z: 8, core: 2. Of those that a mesh axis runs over, the one named last changes fastest.
Arguments:
- query_matrix: bfloat16 [32768, 4096], P(('ctx', 'head')), may hold values from -6 to 6
- key_matrix: bfloat16 [32768, 2048], P(('ctx', 'head')), may hold values from -6 to 6
- value_matrix: bfloat16 [32768, 2048], P(('ctx', 'head')), may hold values from -6 to 6
- documents: int32 [32768], replicated, may hold values from 0 to 46, as said below
- readers: int32 [32, 4], replicated, may hold values from 0 to 1, as said below
Outputs:
- attended: bfloat16 [32768, 4096], P(('ctx', 'head'))
Inputs may be any that keep to these rules, and one draw needn't show every extreme that they name: `documents`: starts at 0 and never falls from one token to the next; it rises by one exactly twice inside every key block other than key blocks 0 to 3 and 12 to 16, and nowhere else. `readers`: every entry of column 0 is 1. Row 0 and rows 12 to 16 are all 1.
All inputs are finite; a program needn't handle non-finite values.
Results may differ from a plain program's by a relative error of at most 0.0038.
Values may be sent and summed in bfloat16 or wider, within the bound.
A program may use at most 192 MiB of HBM per device.

v0:
```python
import jax
import jax.numpy as jnp
from jax import lax
from jax.sharding import PartitionSpec as P

QUERY_HEADS = 32
KEY_VALUE_HEADS = 16
HEAD_WIDTH = 128


score_scale = 168.0 ** (-0.5)
neg_large = -1e30


def passed_along(value, axis, steps):
    count = lax.axis_size(axis)
    leading, last = (max(0, -steps), min(count, count - steps))
    return lax.ppermute(value, axis, [(source, source + steps) for source in range(leading, last)])


def attend_block(running, grouped, block, query_docs, query_pos, key_docs, key_pos, allowed):
    maxima, totals, accumulated = running
    heads_local = block.shape[1] // (2 * HEAD_WIDTH)
    key_part = block[:, : heads_local * HEAD_WIDTH].reshape(block.shape[0], heads_local, HEAD_WIDTH)
    value_part = block[:, heads_local * HEAD_WIDTH :].reshape(
        block.shape[0], heads_local, HEAD_WIDTH
    )
    scores = (
        jnp.einsum("qgmd,kgd->qgmk", grouped, key_part, preferred_element_type=jnp.float32)
        * score_scale
    )
    visible = (
        (query_docs[:, None] == key_docs[None, :])
        & (key_pos[None, :] <= query_pos[:, None])
        & allowed
    )
    visible = visible[:, None, None, :]
    scores = jnp.where(visible, scores, neg_large)
    new_max = jnp.maximum(maxima, jnp.max(scores, axis=3))
    weights = jnp.where(visible, jnp.exp(scores - new_max[..., None]), 0.0)
    rescale = jnp.exp(maxima - new_max)
    totals = totals * rescale + jnp.sum(weights, axis=3)
    product = jnp.einsum(
        "qgmk,kgd->qgmd",
        weights.astype(jnp.bfloat16),
        value_part,
        preferred_element_type=jnp.float32,
    )
    accumulated = accumulated * rescale[..., None] + product
    return (new_max, totals, accumulated)


def per_device(query_matrix, key_matrix, value_matrix, documents, readers):
    query_local, key_local, value_local = (
        lax.all_to_all(query_matrix, "head", split_axis=1, concat_axis=0, tiled=True),
        lax.all_to_all(key_matrix, "head", split_axis=1, concat_axis=0, tiled=True),
        lax.all_to_all(value_matrix, "head", split_axis=1, concat_axis=0, tiled=True),
    )
    rows_per_block = query_local.shape[0]
    heads_local = key_local.shape[1] // HEAD_WIDTH
    query_group_width = QUERY_HEADS // KEY_VALUE_HEADS
    window = readers.shape[1]
    shard_index = lax.axis_index("ctx")
    stacked = jnp.concatenate([key_local, value_local], axis=1)
    block_list = [stacked] + [
        passed_along(stacked, "ctx", distance) for distance in range(1, window)
    ]
    query_start = shard_index * rows_per_block
    row_iota = jnp.arange(rows_per_block, dtype=jnp.int32)
    query_pos = query_start + row_iota
    query_docs = lax.dynamic_slice_in_dim(documents, query_start, rows_per_block)
    grouped = query_local.reshape(rows_per_block, heads_local, query_group_width, HEAD_WIDTH)
    running = (
        jnp.full((rows_per_block, heads_local, query_group_width), neg_large, jnp.float32),
        jnp.zeros((rows_per_block, heads_local, query_group_width), jnp.float32),
        jnp.zeros((rows_per_block, heads_local, query_group_width, HEAD_WIDTH), jnp.float32),
    )
    for distance in range(window):
        owner_block = shard_index - distance
        safe_owner = jnp.maximum(owner_block, 0)
        key_pos = owner_block * rows_per_block + row_iota
        key_docs = lax.dynamic_slice_in_dim(documents, safe_owner * rows_per_block, rows_per_block)
        allowed = (owner_block >= 0) & (readers[safe_owner, distance] > 0)
        running = attend_block(
            running,
            grouped,
            block_list[distance],
            query_docs,
            query_pos,
            key_docs,
            key_pos,
            allowed,
        )
    maxima, totals, accumulated = running
    outputs = (
        (accumulated / totals[..., None])
        .astype(jnp.bfloat16)
        .reshape(rows_per_block, heads_local * query_group_width * HEAD_WIDTH)
    )
    return lax.all_to_all(outputs, "head", split_axis=0, concat_axis=1, tiled=True)


def solution(mesh):
    placed = (
        P(("ctx", "head"), None),
        P(("ctx", "head"), None),
        P(("ctx", "head"), None),
        P(),
        P(),
    )
    return jax.shard_map(
        per_device, mesh=mesh, in_specs=placed, out_specs=P(("ctx", "head"), None), check_vma=False
    )
```

profile of v0, /device:TPU:153, one launch (start us, length us, event | category | flops | bytes accessed | tf_op | source)
XLA Modules:
  0.0 215.4 jit_solution(4050076900092081925)
XLA Ops:
  0.0 2.0 copy.57
  2.0 5.0 %all-to-all-start = ((bf16[128,8,256]{0,2,1:T(8,128)(2,1)}), bf16[128,8,256]{0,2,1:T(8,128)(2,1)S(1)}, u32[]{:S(2)}, u32[]{:S(2)}) async-start(bf16[128,8,256]{0,2,1:T(8,128)(2,1)} %bitcast.1), calls=%async_computation | async-start | bytes 1048576 | tf_op jit(solution)/shard_map/all_to_all | solution.py:56
  7.0 1.5 constant_dynamic-slice_fusion.3
  11.0 2.0 copy.63
  13.0 2.3 %copy.59 = bf16[128,4096]{0,1:T(8,128)(2,1)} copy(bf16[128,4096]{1,0:T(8,128)(2,1)} %param.5) | data formatting | bytes 2097152 | tf_op args[0]
  15.3 0.0 all-to-all-done
  15.3 5.4 %all-to-all-start.2 = ((bf16[128,8,256]{0,2,1:T(8,128)(2,1)}), bf16[128,8,256]{0,2,1:T(8,128)(2,1)S(1)}, u32[]{:S(2)}, u32[]{:S(2)}) async-start(bf16[128,8,256]{0,2,1:T(8,128)(2,1)} %bitcast.7), calls=%async_computation.2 | async-start | bytes 1048576 | tf_op jit(solution)/shard_map/all_to_all | solution.py:57
  20.8 0.8 fusion.52
  21.5 0.9 bitcast_dynamic-update-slice_fusion.1
  22.4 6.0 %all-to-all-done.2 = bf16[128,8,256]{0,2,1:T(8,128)(2,1)S(1)} async-done(((bf16[128,8,256]{0,2,1:T(8,128)(2,1)}), bf16[128,8,256]{0,2,1:T(8,128)(2,1)S(1)}, u32[]{:S(2)}, u32[]{:S(2)}) %all-to-all-start.2) | async-done | bytes 524320 | tf_op jit(solution)/shard_map/all_to_all | solution.py:57
  28.4 6.8 %all-to-all-start.1 = ((bf16[128,8,512]{0,2,1:T(8,128)(2,1)}), bf16[128,8,512]{0,2,1:T(8,128)(2,1)}, u32[]{:S(2)}, u32[]{:S(2)}) async-start(bf16[128,8,512]{0,2,1:T(8,128)(2,1)} %bitcast.4), calls=%async_computation.1 | async-start | bytes 2097152 | tf_op jit(solution)/shard_map/all_to_all | solution.py:55
  35.2 0.9 bitcast_dynamic-update-slice_fusion
  36.1 4.6 %collective-permute-start.1 = (bf16[1024,512]{0,1:T(8,128)(2,1)}, bf16[1024,512]{0,1:T(8,128)(2,1)}, u32[]{:S(2)}, u32[]{:S(2)}) collective-permute-start(bf16[1024,512]{0,1:T(8,128)(2,1)} %bitcast_dynamic-update-slice_fusion), channel_id=1, source_target_pairs={{0,2},{1,3},{2,4},{3,5},{4,6},{5,7},{6,8},{7,9},{8,10},{9,11},{10,... | collective-permute-start | bytes 3145736 | tf_op jit(solution)/shard_map/ppermute | solution.py:18
  40.7 5.4 %and_and_fusion.3 = (pred[1024,1024]{0,1:T(8,128)(4,1)}, pred[1024,1024]{0,1:T(8,128)(4,1)S(1)}, pred[1024,1024]{0,1:T(8,128)(4,1)S(1)}, pred[1024,1024]{0,1:T(8,128)(4,1)}) fusion(s32[1024]{0:T(1024)S(1)} %iota_add_fusion.3, s32[1024]{0:T(1024)S(1)} %get-tuple-element.20, s32[1024]{0:T(1024)S(1)} %get-tuple-element.18, pred[]{:T(512)S(6)} %and.82, ...), kind=kLoop, calls=%fused_computation.31 | loop fusion | flops 16777216 | bytes 4231172 | tf_op jit(solution)/shard_map/and | solution.py:33
  46.1 3.2 %collective-permute-start.2 = (bf16[1024,512]{0,1:T(8,128)(2,1)}, bf16[1024,512]{0,1:T(8,128)(2,1)}, u32[]{:S(2)}, u32[]{:S(2)}) collective-permute-start(bf16[1024,512]{0,1:T(8,128)(2,1)} %bitcast_dynamic-update-slice_fusion), channel_id=1, source_target_pairs={{0,3},{1,4},{2,5},{3,6},{4,7},{5,8},{6,9},{7,10},{8,11},{9,12},{10... | collective-permute-start | bytes 3145736 | tf_op jit(solution)/shard_map/ppermute | solution.py:18
  49.3 2.5 %collective-permute-start = (bf16[1024,512]{0,1:T(8,128)(2,1)}, bf16[1024,512]{0,1:T(8,128)(2,1)}, u32[]{:S(2)}, u32[]{:S(2)}) collective-permute-start(bf16[1024,512]{0,1:T(8,128)(2,1)} %bitcast_dynamic-update-slice_fusion), channel_id=1, source_target_pairs={{0,1},{1,2},{2,3},{3,4},{4,5},{5,6},{6,7},{7,8},{8,9},{9,10},{10,1... | collective-permute-start | bytes 3145736 | tf_op jit(solution)/shard_map/ppermute | solution.py:18
  51.8 1.1 copy.58
  53.0 2.1 reshape.334
  55.1 0.3 copy.64
  55.4 1.0 reshape.336
  56.4 0.0 all-to-all-done.1
  56.4 1.9 copy.60
  58.4 1.3 reshape.335
  59.6 0.0 copy-start.1
  59.6 10.8 %fusion = (f32[1024,2,2]{0,2,1:T(2,128)S(1)}, f32[2,1024,1024,2]{2,1,3,0:T(8,128)}) fusion(pred[1024,1024]{0,1:T(8,128)(4,1)} %get-tuple-element.25, bf16[1024,2,2,128]{0,3,2,1:T(8,128)(2,1)} %reshape.335, bf16[1024,2,128]{0,2,1:T(8,128)(2,1)} %reshape.334), kind=kOutput, calls=%fused_computation.8 | convolution fusion | flops 1086320640 | bytes 19415040 | tf_op jit(solution)/shard_map/qgmd,kgd->qgmk/dot_general | solution.py:29
  70.4 0.0 collective-permute-done.1
  70.4 2.1 fusion.51
  72.5 0.0 copy-done.1
  72.5 7.5 %fusion.2 = (f32[1024,2,2]{0,2,1:T(2,128)S(1)}, f32[2,1024,1024,2]{2,1,3,0:T(8,128)}) fusion(pred[1024,1024]{0,1:T(8,128)(4,1)S(1)} %get-tuple-element.26, bf16[1024,2,128,1]{0,2,3,1:T(8,128)(2,1)S(1)} %bitcast.168, bf16[1024,2,2,128]{0,3,2,1:T(8,128)(2,1)S(1)} %copy-done.1), kind=kOutput, calls=%fused_computation.10 | convolution fusion | flops 1086320640 | bytes 19415040 | tf_op jit(solution)/shard_map/qgmd,kgd->qgmk/dot_general | solution.py:29
  80.0 0.0 copy-start
  80.0 0.0 collective-permute-done.2
  80.0 2.1 fusion.49
  82.2 7.5 %fusion.3 = (f32[1024,2,2]{0,2,1:T(2,128)S(1)}, f32[2,1024,1024,2]{2,1,3,0:T(8,128)}) fusion(pred[1024,1024]{0,1:T(8,128)(4,1)S(1)} %get-tuple-element.27, bf16[1024,2,128,1]{0,2,3,1:T(8,128)(2,1)S(1)} %bitcast.169, bf16[1024,2,2,128]{0,3,2,1:T(8,128)(2,1)S(1)} %copy-done.1), kind=kOutput, calls=%fused_computation.11 | convolution fusion | flops 1086320640 | bytes 19415040 | tf_op jit(solution)/shard_map/qgmd,kgd->qgmk/dot_general | solution.py:29
  89.7 22.2 %collective-permute-done = bf16[1024,512]{0,1:T(8,128)(2,1)} collective-permute-done((bf16[1024,512]{0,1:T(8,128)(2,1)}, bf16[1024,512]{0,1:T(8,128)(2,1)}, u32[]{:S(2)}, u32[]{:S(2)}) %collective-permute-start) | collective-permute-done | bytes 1048608 | tf_op jit(solution)/shard_map/ppermute | solution.py:18
  112.0 2.1 fusion.50
  114.0 0.0 copy-done
  114.0 7.5 %fusion.1 = (f32[1024,2,2]{0,2,1:T(2,128)S(1)}, f32[2,1024,1024,2]{2,1,3,0:T(8,128)}) fusion(pred[1024,1024]{0,1:T(8,128)(4,1)S(1)} %copy-done, bf16[1024,2,128,1]{0,2,3,1:T(8,128)(2,1)S(1)} %bitcast.167, bf16[1024,2,2,128]{0,3,2,1:T(8,128)(2,1)S(1)} %copy-done.1), kind=kOutput, calls=%fused_computation.9 | convolution fusion | flops 1086320640 | bytes 19415040 | tf_op jit(solution)/shard_map/qgmd,kgd->qgmk/dot_general | solution.py:29
  121.6 13.5 %fusion.18 = f32[2,1024,2,128]{3,1,2,0:T(8,128)} fusion(f32[2,1024,1024,2]{2,1,3,0:T(8,128)} %get-tuple-element.40, f32[1024,2,2]{0,2,1:T(2,128)S(1)} %get-tuple-element.24, pred[1024,1024]{0,1:T(8,128)(4,1)} %get-tuple-element.25, bf16[1024,2,128]{0,2,1:T(8,128)(2,1)} %reshape.336), kind=kOutput, calls=%fused_computation.23 | convolution fusion | flops 1094713344 | bytes 20463616 | tf_op jit(solution)/shard_map/qgmk,kgd->qgmd/dot_general | solution.py:43
  135.2 0.0 copy-start.4
  135.2 14.0 %fusion.4 = (f32[1024,2,2]{0,2,1:T(2,128)S(1)}, f32[1024,2,2]{0,2,1:T(2,128)S(1)}) fusion(f32[2,1024,1024,2]{2,1,3,0:T(8,128)} %get-tuple-element.40, f32[1024,2,2]{0,2,1:T(2,128)S(1)} %get-tuple-element.24, pred[1024,1024]{0,1:T(8,128)(4,1)} %get-tuple-element.25, f32[1024,2,2]{0,2,1:T(2,128)S(1)} %get-tuple-element.11, ...), kind=kLoop, calls=%fused_computation.12 | loop fusion | flops 41934848 | bytes 35717120 | tf_op jit(solution)/shard_map/reduce_sum | solution.py:42
  149.2 0.0 copy-done.4
  149.2 0.0 copy-start.3
  149.2 10.7 %fusion.16 = f32[2,128,1024,2]{1,2,3,0:T(8,128)} fusion(bf16[1024,2,128,1]{0,2,3,1:T(8,128)(2,1)S(1)} %bitcast.166, f32[2,1024,1024,2]{2,1,3,0:T(8,128)} %get-tuple-element.38, f32[1024,2,2]{0,2,1:T(2,128)S(1)} %get-tuple-element.11, pred[1024,1024]{0,1:T(8,128)(4,1)S(1)} %copy-done), kind=kOutput, calls=%fused_computation.22 | convolution fusion | flops 1094713344 | bytes 20463616 | tf_op jit(solution)/shard_map/qgmk,kgd->qgmd/dot_general | solution.py:43
  159.9 0.0 copy-done.3
  159.9 0.0 slice-start
  159.9 11.0 %fusion.14 = f32[2,128,1024,2]{1,2,3,0:T(8,128)} fusion(bf16[1024,2,128,1]{0,2,3,1:T(8,128)(2,1)S(1)} %bitcast.165, f32[2,1024,1024,2]{2,1,3,0:T(8,128)} %get-tuple-element.36, f32[1024,2,2]{0,2,1:T(2,128)S(1)} %get-tuple-element.10, pred[1024,1024]{0,1:T(8,128)(4,1)S(1)} %get-tuple-element.26), kind=kOutput, calls=%fused_computation.21 | convolution fusion | flops 1094713344 | bytes 20463616 | tf_op jit(solution)/shard_map/qgmk,kgd->qgmd/dot_general | solution.py:43
  170.9 0.0 copy-start.6
  170.9 0.0 copy-start.7
  170.9 14.7 %fusion.8 = (f32[1024,2,2]{0,2,1:T(2,128)S(1)}, f32[1024,2,2]{0,2,1:T(2,128)S(1)}) fusion(f32[2,1024,1024,2]{2,1,3,0:T(8,128)} %get-tuple-element.36, f32[1024,2,2]{0,2,1:T(2,128)S(1)} %get-tuple-element.10, pred[1024,1024]{0,1:T(8,128)(4,1)S(1)} %get-tuple-element.26, f32[1024,2,2]{0,2,1:T(2,128)S(1)} %get-tuple-element.9, ...), kind=kLoop, calls=%fused_computation.16 | loop fusion | flops 41934848 | bytes 35717120 | tf_op jit(solution)/shard_map/reduce_sum | solution.py:42
  185.6 0.1 multiply_add_fusion
  185.7 0.0 slice-done
  185.7 0.0 slice-done.1
  185.7 0.0 slice-done.2
  185.7 0.0 slice-done.3
  185.7 0.0 copy-done.2
  185.7 0.0 copy-done.5
  185.7 0.0 copy-done.6
  185.8 0.3 copy-done.7
  186.1 8.3 %fusion.25 = bf16[1024,2,2,128]{3,0,2,1:T(8,128)(2,1)S(1)} fusion(f32[2,128,1024,2]{1,2,3,0:T(8,128)S(1)} %copy-done.7, f32[2,128,1024,2]{1,2,3,0:T(8,128)S(1)} %copy-done.6, f32[2,1024,2,128]{3,1,2,0:T(8,128)S(1)} %copy-done.5, bf16[1024,2,128,1]{0,2,3,1:T(8,128)(2,1)S(1)} %bitcast.164, f32[2,1024,1024,2]{2,1,3,0:T(8,128)S(1)} %bitcast.158, ...), kind=kOutput, calls=%fused_computation.34 | convolution fusion | flops 1099431936 | bytes 25788416 | tf_op jit(solution)/shard_map/qgmk,kgd->qgmd/dot_general | solution.py:43
  194.4 0.5 copy.81
  194.9 0.3 copy.115
  195.2 0.1 copy.82
  195.4 18.7 %all_to_all.73 = bf16[8,128,512]{1,2,0:T(8,128)(2,1)S(1)} all-to-all(bf16[8,128,512]{1,2,0:T(8,128)(2,1)S(1)} %copy.82), channel_id=1, replica_groups=mesh['head'=8,'ctx'=32] {'head'}, dimensions={0} | all-to-all | bytes 2097152 | tf_op jit(solution)/shard_map/all_to_all | solution.py:100
  214.1 1.3 copy.83
  (11 shorter events, 0.1 us)
Async XLA Ops:
  2.0 13.3 %all-to-all-start = ((bf16[128,8,256]{0,2,1:T(8,128)(2,1)}), bf16[128,8,256]{0,2,1:T(8,128)(2,1)S(1)}, u32[]{:S(2)}, u32[]{:S(2)}) async-start(bf16[128,8,256]{0,2,1:T(8,128)(2,1)} %bitcast.1), calls=%async_computation | async-start | bytes 1048576 | tf_op jit(solution)/shard_map/all_to_all | solution.py:56
  15.3 13.1 %all-to-all-start.2 = ((bf16[128,8,256]{0,2,1:T(8,128)(2,1)}), bf16[128,8,256]{0,2,1:T(8,128)(2,1)S(1)}, u32[]{:S(2)}, u32[]{:S(2)}) async-start(bf16[128,8,256]{0,2,1:T(8,128)(2,1)} %bitcast.7), calls=%async_computation.2 | async-start | bytes 1048576 | tf_op jit(solution)/shard_map/all_to_all | solution.py:57
  28.4 28.0 %all-to-all-start.1 = ((bf16[128,8,512]{0,2,1:T(8,128)(2,1)}), bf16[128,8,512]{0,2,1:T(8,128)(2,1)}, u32[]{:S(2)}, u32[]{:S(2)}) async-start(bf16[128,8,512]{0,2,1:T(8,128)(2,1)} %bitcast.4), calls=%async_computation.1 | async-start | bytes 2097152 | tf_op jit(solution)/shard_map/all_to_all | solution.py:55
  36.1 34.3 %collective-permute-start.1 = (bf16[1024,512]{0,1:T(8,128)(2,1)}, bf16[1024,512]{0,1:T(8,128)(2,1)}, u32[]{:S(2)}, u32[]{:S(2)}) collective-permute-start(bf16[1024,512]{0,1:T(8,128)(2,1)} %bitcast_dynamic-update-slice_fusion), channel_id=1, source_target_pairs={{0,2},{1,3},{2,4},{3,5},{4,6},{5,7},{6,8},{7,9},{8,10},{9,11},{10,... | collective-permute-start | bytes 3145736 | tf_op jit(solution)/shard_map/ppermute | solution.py:18
  46.1 33.9 %collective-permute-start.2 = (bf16[1024,512]{0,1:T(8,128)(2,1)}, bf16[1024,512]{0,1:T(8,128)(2,1)}, u32[]{:S(2)}, u32[]{:S(2)}) collective-permute-start(bf16[1024,512]{0,1:T(8,128)(2,1)} %bitcast_dynamic-update-slice_fusion), channel_id=1, source_target_pairs={{0,3},{1,4},{2,5},{3,6},{4,7},{5,8},{6,9},{7,10},{8,11},{9,12},{10... | collective-permute-start | bytes 3145736 | tf_op jit(solution)/shard_map/ppermute | solution.py:18
  49.3 62.6 %collective-permute-start = (bf16[1024,512]{0,1:T(8,128)(2,1)}, bf16[1024,512]{0,1:T(8,128)(2,1)}, u32[]{:S(2)}, u32[]{:S(2)}) collective-permute-start(bf16[1024,512]{0,1:T(8,128)(2,1)} %bitcast_dynamic-update-slice_fusion), channel_id=1, source_target_pairs={{0,1},{1,2},{2,3},{3,4},{4,5},{5,6},{6,7},{7,8},{8,9},{9,10},{10,1... | collective-permute-start | bytes 3145736 | tf_op jit(solution)/shard_map/ppermute | solution.py:18
  59.6 12.9 %copy-start.1 = (bf16[1024,2,2,128]{0,3,2,1:T(8,128)(2,1)S(1)}, bf16[1024,2,2,128]{0,3,2,1:T(8,128)(2,1)}, u32[]{:S(2)}) copy-start(bf16[1024,2,2,128]{0,3,2,1:T(8,128)(2,1)} %reshape.335) | copy-start | bytes 3145732
  80.0 34.0 %copy-start = (pred[1024,1024]{0,1:T(8,128)(4,1)S(1)}, pred[1024,1024]{0,1:T(8,128)(4,1)}, u32[]{:S(2)}) copy-start(pred[1024,1024]{0,1:T(8,128)(4,1)} %get-tuple-element.28) | copy-start | bytes 3145732
  135.2 14.0 %copy-start.4 = (bf16[1024,256]{0,1:T(8,128)(2,1)S(1)}, bf16[1024,256]{0,1:T(8,128)(2,1)}, u32[]{:S(2)}) copy-start(bf16[1024,256]{0,1:T(8,128)(2,1)} %get-tuple-element.14) | copy-start | bytes 1572868
  149.2 10.7 %copy-start.3 = (bf16[1024,256]{0,1:T(8,128)(2,1)S(1)}, bf16[1024,256]{0,1:T(8,128)(2,1)}, u32[]{:S(2)}) copy-start(bf16[1024,256]{0,1:T(8,128)(2,1)} %get-tuple-element.17) | copy-start | bytes 1572868
  159.9 25.8 %slice-start = ((s8[16777216]{0:T(1024)(128)(4,1)}), s8[4194304]{0:T(1024)(128)(4,1)S(1)}, s32[]{:S(2)}) async-start(s8[16777216]{0:T(1024)(128)(4,1)} %bitcast.157), calls=%async_computation.4 | async-start | bytes 8388608
  159.9 25.8 %slice-start.1 = ((s8[16777216]{0:T(1024)(128)(4,1)}), s8[4194304]{0:T(1024)(128)(4,1)S(1)}, s32[]{:S(2)}) async-start(s8[16777216]{0:T(1024)(128)(4,1)} %bitcast.157), calls=%async_computation.5 | async-start | bytes 8388608
  170.9 14.8 %slice-start.2 = ((s8[16777216]{0:T(1024)(128)(4,1)}), s8[4194304]{0:T(1024)(128)(4,1)S(1)}, s32[]{:S(2)}) async-start(s8[16777216]{0:T(1024)(128)(4,1)} %bitcast.157), calls=%async_computation.6 | async-start | bytes 8388608
  170.9 14.8 %slice-start.3 = ((s8[16777216]{0:T(1024)(128)(4,1)}), s8[4194304]{0:T(1024)(128)(4,1)S(1)}, s32[]{:S(2)}) async-start(s8[16777216]{0:T(1024)(128)(4,1)} %bitcast.157), calls=%async_computation.7 | async-start | bytes 8388608
  170.9 14.8 %copy-start.2 = (bf16[1024,256]{0,1:T(8,128)(2,1)S(1)}, bf16[1024,256]{0,1:T(8,128)(2,1)}, u32[]{:S(2)}) copy-start(bf16[1024,256]{0,1:T(8,128)(2,1)} %get-tuple-element.12) | copy-start | bytes 1572868
  170.9 14.8 %copy-start.5 = (f32[2,1024,2,128]{3,1,2,0:T(8,128)S(1)}, f32[2,1024,2,128]{3,1,2,0:T(8,128)}, u32[]{:S(2)}) copy-start(f32[2,1024,2,128]{3,1,2,0:T(8,128)} %fusion.18) | copy-start | bytes 6291460
  170.9 14.8 %copy-start.6 = (f32[2,128,1024,2]{1,2,3,0:T(8,128)S(1)}, f32[2,128,1024,2]{1,2,3,0:T(8,128)}, u32[]{:S(2)}) copy-start(f32[2,128,1024,2]{1,2,3,0:T(8,128)} %fusion.16) | copy-start | bytes 6291460
  170.9 15.1 %copy-start.7 = (f32[2,128,1024,2]{1,2,3,0:T(8,128)S(1)}, f32[2,128,1024,2]{1,2,3,0:T(8,128)}, u32[]{:S(2)}) copy-start(f32[2,128,1024,2]{1,2,3,0:T(8,128)} %fusion.14) | copy-start | bytes 6291460
where the time goes:
time: 218 us; the launch traced here: 215 us
  matrix products  77 us (35%)
  other arithmetic  34.2 us (16%)
  waiting for transfers between devices  28.3 us (13%)
  starting transfers between devices  27.6 us (13%)
  local copies, waits for them, and re-layouts  27 us (12%)
  blocking collectives  18.7 us (9%)
  between operations  2.72 us (1%)
    dot_general x4, matrix products, attend_block(): jnp.einsum('qgmk,kgd->qgmd', weights.astype(jnp.bfloat16), value_part, pr...  43.6 us
    dot_general x4, matrix products, attend_block(): jnp.einsum('qgmd,kgd->qgmk', grouped, key_part, preferred_element_type=jn...  33.4 us
    reduce_sum x2, other arithmetic, attend_block(): totals = totals * rescale + jnp.sum(weights, axis=3)  28.7 us
    ppermute x3, waiting for transfers between devices, passed_along(): lax.ppermute(value, axis, [(source, source + steps) for source in range(l...  22.2 us
    all_to_all x1, blocking collectives, per_device(): lax.all_to_all(outputs, 'head', split_axis=0, concat_axis=1, tiled=True)  18.7 us
    ppermute x3, starting transfers between devices, passed_along(): lax.ppermute(value, axis, [(source, source + steps) for source in range(l...  10.4 us
    unnamed x29, local copies, waits for them, and re-layouts  7.82 us
    all_to_all x1, starting transfers between devices, per_device(): lax.all_to_all(query_matrix, 'head', split_axis=1, concat_axis=0, tiled=T...  6.81 us
  transfers between devices with their start and end apart: 6, of which 2 were waited for; matrix products, arithmetic and copies ran while one was open for 24% of the time, Pallas kernels for 0%

commit v1 on v0

v1 whole, which is shorter than its diff:
```python
import jax
import jax.numpy as jnp
from jax import lax
from jax.experimental import pallas as pl
from jax.experimental.pallas import tpu as pltpu
from jax.sharding import PartitionSpec as P

QUERY_HEADS = 32
KEY_VALUE_HEADS = 16
HEAD_WIDTH = 128
WIN = 4
BLOCK = 1024
TOK_DEV = 128
SIDE = 4
SLOTS = SIDE + WIN - 1
TILE = 512
CHUNK = 512

SCALE = 168.0**-0.5 * 1.4426950408889634
STEP = 16384.0
READER_ROW = 64

MESH = pl.DeviceIdType.MESH


def rows_of(start, size):
    return pl.ds(pl.multiple_of(start, TOK_DEV), size)


def columns_of(head):
    return pl.ds(pl.multiple_of(head * HEAD_WIDTH, HEAD_WIDTH), HEAD_WIDTH)


def kernel(
    readers, q_in, k_in, v_in, documents,
    out,
    q_held, k_held, v_held, q_mask, k_mask, q_wide, scores, peak, total, o_held,
    local_sem, send_sem, q_sem, kv_sem, twin_sem, halo_sem, halo_twin_sem, out_sem,
):
    head_index = lax.axis_index("head")
    ctx_index = lax.axis_index("ctx")
    y, core = head_index // 2, head_index % 2
    z, x = ctx_index // SIDE, ctx_index % SIDE
    planes = lax.axis_size("ctx") // SIDE
    chip = x * SIDE + y
    twin = {"head": y * 2 + 1 - core, "ctx": ctx_index}
    up = {"head": head_index, "ctx": ctx_index + SIDE}

    def device(dx, dy, dc):
        return (x + dx) % SIDE, (y + dy) % SIDE, (core + dc) % 2

    def target(X, Y, C):
        return {"head": Y * 2 + C, "ctx": z * SIDE + X}

    barrier = pltpu.get_barrier_semaphore()

    def greet(i, carry):
        X, Y, C = device(i // 8, (i // 2) % 4, i % 2)
        pl.semaphore_signal(barrier, inc=1, device_id=target(X, Y, C), device_id_type=MESH)
        return carry

    lax.fori_loop(1, 2 * SIDE * SIDE, greet, 0)

    @pl.when(z + 1 < planes)
    def _():
        pl.semaphore_signal(barrier, inc=1, device_id=up, device_id_type=MESH)

    @pl.when(z > 0)
    def _():
        pl.semaphore_signal(
            barrier, inc=1, device_id={"head": head_index, "ctx": ctx_index - SIDE}, device_id_type=MESH
        )

    neighbours = jnp.where(z > 0, 1, 0) + jnp.where(z + 1 < planes, 1, 0)
    pl.semaphore_wait(barrier, 2 * SIDE * SIDE - 1 + neighbours)

    own_row = x * BLOCK + head_index * TOK_DEV
    halo_rows = (WIN - 1) * BLOCK
    kv_pairs = ((k_in, k_held, 0), (v_in, v_held, 1))

    def remote(src, dst, recv, where):
        return pltpu.make_async_remote_copy(
            src_ref=src, dst_ref=dst, send_sem=send_sem, recv_sem=recv, device_id=where, device_id_type=MESH
        )

    own_copies = [
        pltpu.make_async_copy(src.at[:, columns_of(chip)], dst.at[rows_of(halo_rows + own_row, TOK_DEV)], local_sem.at[n])
        for src, dst, n in kv_pairs
    ] + [
        pltpu.make_async_copy(
            q_in.at[:, columns_of(chip * 2 + core)], q_held.at[rows_of(own_row, TOK_DEV)], local_sem.at[2]
        )
    ]
    for copy in own_copies:
        copy.start()
    for src, dst, _ in kv_pairs:
        remote(src.at[:, columns_of(chip)], dst.at[rows_of(halo_rows + own_row, TOK_DEV)], twin_sem, twin).start()

    def offset(i):
        return (i + i // SIDE) % SIDE, i % SIDE

    def send_kv(i, carry):
        dx, dy = offset(i)
        X, Y, C = device(dx, dy, 0)
        for src, dst, n in kv_pairs:
            remote(
                src.at[:, columns_of(X * SIDE + Y)],
                dst.at[rows_of(halo_rows + own_row, TOK_DEV)],
                kv_sem.at[n, i],
                target(X, Y, C),
            ).start()
        return carry

    lax.fori_loop(1, SIDE * SIDE, send_kv, 0)

    def send_q(i, carry):
        dx, dy = offset(i // 2)
        X, Y, C = device(dx, dy, i % 2)
        remote(
            q_in.at[:, columns_of((X * SIDE + Y) * 2 + C)],
            q_held.at[rows_of(own_row, TOK_DEV)],
            q_sem,
            target(X, Y, C),
        ).start()
        return carry


    lane = lax.broadcasted_iota(jnp.int32, (TOK_DEV, HEAD_WIDTH), 1)

    def document_columns(group):
        row = documents[pl.ds(group, 1), :]
        return jnp.transpose(jnp.broadcast_to(row, (TOK_DEV, TOK_DEV)))

    def key_mask(slot, carry):
        block = z * SIDE + slot - (WIN - 1)
        safe = jnp.maximum(block, 0)
        permit = jnp.full((TOK_DEV, HEAD_WIDTH), -STEP, jnp.float32)
        for j in range(SIDE):
            distance = j + (WIN - 1) - slot
            inside = (distance >= 0) & (distance < WIN) & (block >= 0)
            value = readers[jnp.clip(distance, 0, WIN - 1), safe]
            value = jnp.where(inside & (value > 0), 0.0, -STEP)
            permit = jnp.where(lane == READER_ROW + j, value, permit)

        def group_mask(g, inner):
            same = document_columns(safe * (BLOCK // TOK_DEV) + g) == lane
            k_mask[rows_of(slot * BLOCK + g * TOK_DEV, TOK_DEV), :] = jnp.where(same, 0.0, permit).astype(jnp.bfloat16)
            return inner

        return lax.fori_loop(0, BLOCK // TOK_DEV, group_mask, carry)

    lax.fori_loop(0, SLOTS, key_mask, 0)

    def query_mask(g, carry):
        j = g // (BLOCK // TOK_DEV)
        chosen = (document_columns(z * SIDE * (BLOCK // TOK_DEV) + g) == lane) | (lane == READER_ROW + j)
        q_mask[rows_of(g * TOK_DEV, TOK_DEV), :] = jnp.where(chosen, 1.0, 0.0).astype(jnp.bfloat16)
        return carry

    lax.fori_loop(0, SIDE * BLOCK // TOK_DEV, query_mask, 0)

    own_block = z * SIDE

    def whole(b):
        return (b < 4) | ((b >= 12) & (b <= 16))

    def pass_on(i, carry):
        dx, dy = offset(i)
        X, Y, C = device(SIDE - dx, SIDE - dy, 0)
        row = halo_rows + X * BLOCK + (Y * 2 + core) * TOK_DEV
        for _, dst, n in kv_pairs:
            piece = dst.at[rows_of(row, TOK_DEV)]
            pltpu.make_async_copy(piece, piece, kv_sem.at[n, i]).wait()
            remote(piece, piece, twin_sem, twin).start()
        return carry

    def to_next_plane(X, Y):
        row = halo_rows + X * BLOCK + (Y * 2 + core) * TOK_DEV
        beyond = (X - 1) * BLOCK + (Y * 2 + core) * TOK_DEV
        for _, dst, _ in kv_pairs:
            remote(dst.at[rows_of(row, TOK_DEV)], dst.at[rows_of(beyond, TOK_DEV)], halo_sem.at[X - 1], up).start()

    def reads_halo(plane, slot):
        first = plane * SIDE
        near = (plane > 0) & (slot == 2)
        far = (plane > 0) & whole(first - 1) & whole(first - 2)
        return near | far

    def wait_rows(rows, sem):
        view = q_held.at[pl.ds(0, rows)]
        pltpu.make_async_copy(view, view, sem).wait()

    for copy in own_copies[:2]:
        copy.wait()

    def handle(i, carry):
        dx, dy = offset(i)
        X, Y, C = device(SIDE - dx, SIDE - dy, 0)

        @pl.when(i > 0)
        def _():
            pass_on(i, 0)

        @pl.when((z + 1 < planes) & (X > 0))
        def _():
            @pl.when(reads_halo(z + 1, X - 1))
            def _():
                to_next_plane(X, Y)

        @pl.when(i > 0)
        def _():
            send_q(2 * i, 0)

        send_q(2 * i + 1, 0)
        return carry

    lax.fori_loop(0, SIDE * SIDE, handle, 0)

    def take_halo(slot, carry):
        @pl.when(reads_halo(z, slot))
        def _():
            wait_rows(SIDE * 2 * TOK_DEV, halo_sem.at[slot])
            for Y in range(SIDE):
                row = slot * BLOCK + (Y * 2 + core) * TOK_DEV
                for _, dst, _ in kv_pairs:
                    piece = dst.at[rows_of(row, TOK_DEV)]
                    remote(piece, piece, halo_twin_sem.at[slot], twin).start()

        return carry

    lax.fori_loop(0, WIN - 1, take_halo, 0)
    wait_rows(SIDE * SIDE * 2 * TOK_DEV, twin_sem)

    def halo_here(slot, carry):
        @pl.when(reads_halo(z, slot))
        def _():
            wait_rows(SIDE * 2 * TOK_DEV, halo_twin_sem.at[slot])

        return carry

    lax.fori_loop(0, WIN - 1, halo_here, 0)
    own_copies[2].wait()
    wait_rows((2 * SIDE * SIDE - 1) * TOK_DEV, q_sem)

    head = chip * 2 + core
    row_iota = lax.broadcasted_iota(jnp.int32, (TILE, CHUNK), 0)
    column_iota = lax.broadcasted_iota(jnp.int32, (TILE, CHUNK), 1)

    def attend(t, carry):
        j = (x + 1 + t // 2) % SIDE
        i = t % 2
        b = own_block + j
        one = jnp.where(b >= 1, 1, 0)
        two = jnp.where((b >= 2) & whole(b - 1), 1, 0)
        three = jnp.where((b >= 3) & whole(b - 1) & whole(b - 2), 1, 0)
        before = one + two + three
        row = j * BLOCK + i * TILE
        scaled = q_held[rows_of(row, TILE), :]
        q_wide[:, :HEAD_WIDTH] = scaled
        q_wide[:, HEAD_WIDTH:] = q_mask[rows_of(row, TILE), :]
        start = (WIN - 1 + j - before) * BLOCK
        count = before * (BLOCK // CHUNK) + i

        def score(c):
            rows = rows_of(start + c * CHUNK, CHUNK)
            keys = jnp.concatenate([k_held[rows, :], k_mask[rows, :]], axis=1)
            return SCALE * lax.dot_general(
                q_wide[...], keys, (((1,), (1,)), ((), ())), preferred_element_type=jnp.float32
            )

        def groups(s):
            return [s[:, g * 128 : (g + 1) * 128] for g in range(CHUNK // 128)]

        s = jnp.where(column_iota <= row_iota, score(count), -3.0e38)
        scores[count] = s
        a = groups(s)
        peak[...] = jnp.maximum(jnp.maximum(a[0], a[1]), jnp.maximum(a[2], a[3]))

        def first_pass(c, inner):
            s = score(c)
            scores[c] = s
            a = groups(s)
            peak[...] = jnp.maximum(
                peak[...], jnp.maximum(jnp.maximum(a[0], a[1]), jnp.maximum(a[2], a[3]))
            )
            return inner

        lax.fori_loop(0, count, first_pass, 0)
        peak[...] = jnp.broadcast_to(jnp.max(peak[...], axis=1, keepdims=True), (TILE, 128))
        total[...] = jnp.zeros_like(total)
        ones = jnp.ones((CHUNK, HEAD_WIDTH), jnp.bfloat16)

        def second_pass(c, inner):
            rows = rows_of(start + c * CHUNK, CHUNK)
            m = peak[...]
            p = jnp.concatenate(
                [jnp.exp2(scores[c, :, g * 128 : (g + 1) * 128] - m).astype(jnp.bfloat16) for g in range(CHUNK // 128)],
                axis=1,
            )
            values = jnp.concatenate([v_held[rows, :], ones], axis=1)
            total[...] += jnp.dot(p, values, preferred_element_type=jnp.float32)
            return inner

        lax.fori_loop(0, count + 1, second_pass, 0)
        o_held[rows_of(row, TILE), :] = (total[:, :HEAD_WIDTH] / total[:, HEAD_WIDTH:]).astype(jnp.bfloat16)

        for piece in range(TILE // TOK_DEV):
            place = i * (TILE // TOK_DEV) + piece
            source = o_held.at[rows_of(row + piece * TOK_DEV, TOK_DEV)]
            goal = out.at[:, columns_of(head)]
            mine = (j == x) & (place == head_index)

            @pl.when(mine)
            def _():
                pltpu.make_async_copy(source, goal, local_sem.at[3]).start()

            @pl.when(jnp.logical_not(mine))
            def _():
                remote(source, goal, out_sem, {"head": place, "ctx": z * SIDE + j}).start()

        return carry

    lax.fori_loop(0, 2 * SIDE, attend, 0)

    last = pltpu.make_async_copy(o_held.at[pl.ds(0, TOK_DEV)], out.at[:, pl.ds(0, HEAD_WIDTH)], local_sem.at[3])
    last.wait()
    wait_rows((2 * SIDE * SIDE - 1) * TOK_DEV, out_sem)
    everything = (2 * 15 + 2 * 16 + 31 + 31) * TOK_DEV
    while_left = everything
    step = SIDE * BLOCK
    while while_left > 0:
        part = min(step, while_left)
        wait_rows(part, send_sem)
        while_left -= part

    def sent_up(slot, carry):
        @pl.when(z + 1 < planes)
        def _():
            @pl.when(reads_halo(z + 1, slot))
            def _():
                wait_rows(SIDE * 2 * TOK_DEV, send_sem)

        @pl.when(reads_halo(z, slot))
        def _():
            wait_rows(SIDE * 2 * TOK_DEV, send_sem)

        return carry

    lax.fori_loop(0, WIN - 1, sent_up, 0)


def per_device(query_matrix, key_matrix, value_matrix, documents, readers):
    tokens = SIDE * BLOCK
    window = SLOTS * BLOCK
    return pl.pallas_call(
        kernel,
        out_shape=jax.ShapeDtypeStruct((TOK_DEV, QUERY_HEADS * HEAD_WIDTH), jnp.bfloat16),
        in_specs=[
            pl.BlockSpec(memory_space=pltpu.SMEM),
            pl.BlockSpec(memory_space=pl.ANY),
            pl.BlockSpec(memory_space=pl.ANY),
            pl.BlockSpec(memory_space=pl.ANY),
            pl.BlockSpec(memory_space=pltpu.VMEM),
        ],
        out_specs=pl.BlockSpec(memory_space=pl.ANY),
        scratch_shapes=[
            pltpu.VMEM((tokens, HEAD_WIDTH), jnp.bfloat16),
            pltpu.VMEM((window, HEAD_WIDTH), jnp.bfloat16),
            pltpu.VMEM((window, HEAD_WIDTH), jnp.bfloat16),
            pltpu.VMEM((tokens, HEAD_WIDTH), jnp.bfloat16),
            pltpu.VMEM((window, HEAD_WIDTH), jnp.bfloat16),
            pltpu.VMEM((TILE, 2 * HEAD_WIDTH), jnp.bfloat16),
            pltpu.VMEM((WIN * BLOCK // CHUNK, TILE, CHUNK), jnp.float32),
            pltpu.VMEM((TILE, 128), jnp.float32),
            pltpu.VMEM((TILE, 2 * HEAD_WIDTH), jnp.float32),
            pltpu.VMEM((tokens, HEAD_WIDTH), jnp.bfloat16),
            pltpu.SemaphoreType.DMA((4,)),
            pltpu.SemaphoreType.DMA,
            pltpu.SemaphoreType.DMA,
            pltpu.SemaphoreType.DMA((2, SIDE * SIDE)),
            pltpu.SemaphoreType.DMA,
            pltpu.SemaphoreType.DMA((WIN - 1,)),
            pltpu.SemaphoreType.DMA((WIN - 1,)),
            pltpu.SemaphoreType.DMA,
        ],
        compiler_params=pltpu.CompilerParams(
            collective_id=0, has_side_effects=True, vmem_limit_bytes=60 * 1024 * 1024
        ),
    )(readers.T, query_matrix, key_matrix, value_matrix, documents.reshape(-1, 128))


def solution(mesh):
    placed = (
        P(("ctx", "head"), None),
        P(("ctx", "head"), None),
        P(("ctx", "head"), None),
        P(),
        P(),
    )
    return jax.shard_map(
        per_device, mesh=mesh, in_specs=placed, out_specs=P(("ctx", "head"), None), check_vma=False
    )
```

time: 218 us -> 74.1 us (0.34); the launches traced: 215 us -> 74 us
  matrix products: 77 us -> 0 us
  Pallas kernels: 0 us -> 71.7 us
  other arithmetic: 34.2 us -> 0 us
  waiting for transfers between devices: 28.3 us -> 0 us
  starting transfers between devices: 27.6 us -> 0 us
  local copies, waits for them, and re-layouts: 27 us -> 2.29 us
  blocking collectives: 18.7 us -> 0 us
  between operations: 2.72 us -> 0.01 us
    dot_general x8 -> x0, matrix products: 77 us -> none  [the longest x4 43.6 us: attend_block(): jnp.einsum('qgmk,kgd->qgmd', weights.astype(jnp.bfloat16), value_part, pr...]
    pallas_call x0 -> x1, Pallas kernels: none -> 71.7 us  [per_device(): pl.pallas_call(kernel, out_shape=jax.ShapeDtypeStruct((TOK_DEV, QUERY_HEA...]
    reduce_sum x2 -> x0, other arithmetic: 28.7 us -> none  [attend_block(): totals = totals * rescale + jnp.sum(weights, axis=3)]
    ppermute x3 -> x0, waiting for transfers between devices: 22.2 us -> none  [passed_along(): lax.ppermute(value, axis, [(source, source + steps) for source in range(l...]
    all_to_all x1 -> x0, blocking collectives: 18.7 us -> none  [per_device(): lax.all_to_all(outputs, 'head', split_axis=0, concat_axis=1, tiled=True)]
    all_to_all x3 -> x0, starting transfers between devices: 17.2 us -> none  [the longest x1 6.81 us: per_device(): lax.all_to_all(query_matrix, 'head', split_axis=1, concat_axis=0, tiled=T...]
    ppermute x3 -> x0, starting transfers between devices: 10.4 us -> none  [passed_along(): lax.ppermute(value, axis, [(source, source + steps) for source in range(l...]
    slice x3 -> x0, local copies, waits for them, and re-layouts: 6.28 us -> none  [the longest x2 4.21 us: attend_block(): block[:, heads_local * HEAD_WIDTH:]]
  transfers between devices with their start and end apart: 6 -> 0, of which waited for: 2 -> 0; matrix products, arithmetic and copies ran while one was open for 24% -> 0% of each run, Pallas kernels for 0% -> 0%
where the time goes in v1:
time: 74.1 us; the launch traced here: 74 us
  Pallas kernels  71.7 us (97%)
  local copies, waits for them, and re-layouts  2.29 us (3%)
    pallas_call x1, Pallas kernels, per_device(): pl.pallas_call(kernel, out_shape=jax.ShapeDtypeStruct((TOK_DEV, QUERY_HEA...  71.7 us
    unnamed x1, local copies, waits for them, and re-layouts  2.29 us

profile of v1, /device:TPU:153, one launch (start us, length us, event | category | flops | bytes accessed | tf_op | source)
XLA Modules:
  0.0 74.0 jit_solution(13173554532970631608)
XLA Ops:
  0.0 71.7 %shard_map.55 = bf16[128,4096]{1,0:T(8,128)(2,1)} custom-call(s32[4,32]{1,0:T(4,128)} %bitcast.3, bf16[128,4096]{1,0:T(8,128)(2,1)} %q_in.1, bf16[128,2048]{1,0:T(8,128)(2,1)} %k_in.1, bf16[128,2048]{1,0:T(8,128)(2,1)} %v_in.1, s32[256,128]{1,0:T(8,128)} %bitcast.2), custom_call_target="tpu_custom_call" | custom-call | tf_op jit(solution)/shard_map/pallas_call | solution.py:355
  71.7 2.3 %copy.7 = bf16[128,4096]{1,0:T(8,128)(2,1)} copy(bf16[128,4096]{1,0:T(8,128)(2,1)} %shard_map.55) | data formatting | bytes 2097152

commit v2 on v1

v2 whole, which is shorter than its diff:
```python
import jax
import jax.numpy as jnp
from jax import lax
from jax.experimental import pallas as pl
from jax.experimental.pallas import tpu as pltpu
from jax.sharding import PartitionSpec as P

QUERY_HEADS = 32
KEY_VALUE_HEADS = 16
HEAD_WIDTH = 128
WIN = 4
BLOCK = 1024
N_HEAD = 8
TOK_DEV = 128
SIDE = 4
SLOTS = SIDE + WIN - 1
PART = TOK_DEV // 2
TILE = 256
STRETCH = 1024
EARLY = 20

SCALE = 168.0**-0.5 * 1.4426950408889634
STEP = 16384.0
READER_ROW = 64

MESH = pl.DeviceIdType.MESH


def rows_of(start, size):
    return pl.ds(pl.multiple_of(start, TOK_DEV), size)


def part_rows(start, size):
    return pl.ds(pl.multiple_of(start, PART), size)


def columns_of(head):
    return pl.ds(pl.multiple_of(head * HEAD_WIDTH, HEAD_WIDTH), HEAD_WIDTH)


def kernel(
    readers, q_in, k_in, v_in, documents,
    out,
    q_held, kv_held, q_mask, k_mask, scores, o_held,
    local_sem, send_sem, q_sem, kv_sem, twin_sem, halo_sem, halo_twin_sem, out_sem,
):
    head_index = lax.axis_index("head")
    ctx_index = lax.axis_index("ctx")
    y, core = head_index // 2, head_index % 2
    z, x = ctx_index // SIDE, ctx_index % SIDE
    planes = lax.axis_size("ctx") // SIDE
    chip = x * SIDE + y
    twin = {"head": y * 2 + 1 - core, "ctx": ctx_index}
    up = {"head": head_index, "ctx": ctx_index + SIDE}

    def device(dx, dy, dc):
        return (x + dx) % SIDE, (y + dy) % SIDE, (core + dc) % 2

    def target(X, Y, C):
        return {"head": Y * 2 + C, "ctx": z * SIDE + X}

    barrier = pltpu.get_barrier_semaphore()

    hops = (0, 1, 2, 1)
    far_first = sorted(range(1, 2 * SIDE * SIDE), key=lambda i: -hops[i // 8] - hops[i // 2 % 4])
    for i in far_first:
        X, Y, C = device(i // 8, (i // 2) % 4, i % 2)
        pl.semaphore_signal(barrier, inc=1, device_id=target(X, Y, C), device_id_type=MESH)

    @pl.when(z + 1 < planes)
    def _():
        pl.semaphore_signal(barrier, inc=1, device_id=up, device_id_type=MESH)

    @pl.when(z > 0)
    def _():
        pl.semaphore_signal(
            barrier, inc=1, device_id={"head": head_index, "ctx": ctx_index - SIDE}, device_id_type=MESH
        )

    own_block = z * SIDE
    groups = BLOCK // TOK_DEV
    lane = lax.broadcasted_iota(jnp.int32, (TOK_DEV, HEAD_WIDTH), 1)

    def whole(b):
        return (b < 4) | ((b >= 12) & (b <= 16))

    def reads_halo(plane, slot):
        first = plane * SIDE
        near = (plane > 0) & (slot == 2)
        far = (plane > 0) & whole(first - 1) & whole(first - 2)
        return near | far

    def key_mask(slot, g):
        block = jnp.maximum(own_block + slot - (WIN - 1), 0)
        row = documents[pl.ds(block * groups + g, 1), :]
        same = jnp.transpose(jnp.broadcast_to(row, (TOK_DEV, TOK_DEV))) == lane
        permit = jnp.full((TOK_DEV, HEAD_WIDTH), -STEP, jnp.float32)
        for j in range(SIDE):
            distance = j + (WIN - 1) - slot
            inside = (distance >= 0) & (distance < WIN)
            value = readers[jnp.clip(distance, 0, WIN - 1), block]
            permit = jnp.where(lane == READER_ROW + j, jnp.where(inside & (value > 0), 0.0, -STEP), permit)
        k_mask[rows_of(slot * BLOCK + g * TOK_DEV, TOK_DEV), :] = jnp.where(same, 0.0, permit).astype(jnp.bfloat16)
        return same

    def own_mask(n, carry):
        j, g = n // groups, n % groups
        same = key_mask(WIN - 1 + j, g)
        wanted = jnp.where(same | (lane == READER_ROW + j), 1.0, 0.0).astype(jnp.bfloat16)
        for part in range(2):
            q_mask[part_rows(part * (SIDE * BLOCK // 2) + n * PART, PART), :] = wanted[part * PART : (part + 1) * PART]
        return carry

    lax.fori_loop(0, EARLY, own_mask, 0)

    neighbours = jnp.where(z > 0, 1, 0) + jnp.where(z + 1 < planes, 1, 0)
    pl.semaphore_wait(barrier, 2 * SIDE * SIDE - 1 + neighbours)

    own_row = x * BLOCK + head_index * TOK_DEV
    own_part = (x * N_HEAD + head_index) * PART
    part_size = SIDE * BLOCK // 2
    halo_rows = (WIN - 1) * BLOCK
    kv_pairs = ((k_in, 0), (v_in, 1))

    def remote(src, dst, recv, where):
        return pltpu.make_async_remote_copy(
            src_ref=src, dst_ref=dst, send_sem=send_sem, recv_sem=recv, device_id=where, device_id_type=MESH
        )

    own_copies = [
        pltpu.make_async_copy(
            src.at[:, columns_of(chip)], kv_held.at[n, rows_of(halo_rows + own_row, TOK_DEV)], local_sem.at[n]
        )
        for src, n in kv_pairs
    ] + [
        pltpu.make_async_copy(
            q_in.at[pl.ds(part * PART, PART), columns_of(chip * 2 + core)],
            q_held.at[part_rows(part * part_size + own_part, PART)],
            local_sem.at[2 + part],
        )
        for part in range(2)
    ]
    for copy in own_copies:
        copy.start()
    for src, n in kv_pairs:
        remote(
            src.at[:, columns_of(chip)], kv_held.at[n, rows_of(halo_rows + own_row, TOK_DEV)], twin_sem, twin
        ).start()

    def offset(i):
        return (i + i // SIDE) % SIDE, i % SIDE

    def send_kv(i, carry):
        dx, dy = offset(i)
        X, Y, C = device(dx, dy, 0)
        for src, n in kv_pairs:
            remote(
                src.at[:, columns_of(X * SIDE + Y)],
                kv_held.at[n, rows_of(halo_rows + own_row, TOK_DEV)],
                kv_sem.at[i],
                target(X, Y, C),
            ).start()
        return carry

    lax.fori_loop(1, SIDE * SIDE, send_kv, 0)

    def send_q(i, part):
        dx, dy = offset(i // 2)
        X, Y, C = device(dx, dy, i % 2)
        remote(
            q_in.at[pl.ds(part * PART, PART), columns_of((X * SIDE + Y) * 2 + C)],
            q_held.at[part_rows(part * part_size + own_part, PART)],
            q_sem.at[part],
            target(X, Y, C),
        ).start()


    def pass_on(i, carry):
        dx, dy = offset(i)
        X, Y, C = device(SIDE - dx, SIDE - dy, 0)
        row = halo_rows + X * BLOCK + (Y * 2 + core) * TOK_DEV
        piece = kv_held.at[:, rows_of(row, TOK_DEV)]
        pltpu.make_async_copy(piece, piece, kv_sem.at[i]).wait()
        remote(piece, piece, twin_sem, twin).start()
        return carry

    def to_next_plane(X, Y):
        row = halo_rows + X * BLOCK + (Y * 2 + core) * TOK_DEV
        beyond = (X - 1) * BLOCK + (Y * 2 + core) * TOK_DEV
        remote(
            kv_held.at[:, rows_of(row, TOK_DEV)], kv_held.at[:, rows_of(beyond, TOK_DEV)], halo_sem.at[X - 1], up
        ).start()

    def wait_rows(rows, sem):
        view = q_held.at[pl.ds(0, rows)]
        pltpu.make_async_copy(view, view, sem).wait()

    for copy in own_copies[:2]:
        copy.wait()

    def handle(i, carry):
        dx, dy = offset(i)
        X, Y, C = device(SIDE - dx, SIDE - dy, 0)

        @pl.when(i > 0)
        def _():
            pass_on(i, 0)

        @pl.when((z + 1 < planes) & (X > 0))
        def _():
            @pl.when(reads_halo(z + 1, X - 1))
            def _():
                to_next_plane(X, Y)

        @pl.when(i > 0)
        def _():
            send_q(2 * i, 0)

        send_q(2 * i + 1, 0)

        @pl.when(EARLY + i < SIDE * groups)
        def _():
            own_mask(EARLY + i, 0)

        @pl.when((i >= groups) & reads_halo(z, WIN - 2))
        def _():
            key_mask(WIN - 2, i - groups)

        @pl.when(reads_halo(z, 0))
        def _():
            key_mask(i // groups, i % groups)

        return carry

    lax.fori_loop(0, SIDE * SIDE, handle, 0)

    def send_last(i, carry):
        send_q(i, 1)
        return carry

    lax.fori_loop(1, 2 * SIDE * SIDE, send_last, 0)

    def take_halo(slot, carry):
        @pl.when(reads_halo(z, slot))
        def _():
            wait_rows(SIDE * 2 * TOK_DEV, halo_sem.at[slot])
            for Y in range(SIDE):
                row = slot * BLOCK + (Y * 2 + core) * TOK_DEV
                piece = kv_held.at[:, rows_of(row, TOK_DEV)]
                remote(piece, piece, halo_twin_sem.at[slot], twin).start()

        return carry

    lax.fori_loop(0, WIN - 1, take_halo, 0)
    wait_rows(SIDE * SIDE * 2 * TOK_DEV, twin_sem)

    def halo_here(slot, carry):
        @pl.when(reads_halo(z, slot))
        def _():
            wait_rows(SIDE * 2 * TOK_DEV, halo_twin_sem.at[slot])

        return carry

    lax.fori_loop(0, WIN - 1, halo_here, 0)

    head = chip * 2 + core

    def attend(t, carry):
        part = t // SIDE
        j = (x + 1 + t % SIDE) % SIDE

        @pl.when(t % SIDE == 0)
        def _():
            view = q_held.at[pl.ds(0, PART)]
            pltpu.make_async_copy(view, view, local_sem.at[2 + part]).wait()
            view = q_held.at[pl.ds(0, (2 * SIDE * SIDE - 1) * PART)]
            pltpu.make_async_copy(view, view, q_sem.at[part]).wait()

        b = own_block + j
        one = jnp.where(b >= 1, 1, 0)
        two = jnp.where((b >= 2) & whole(b - 1), 1, 0)
        three = jnp.where((b >= 3) & whole(b - 1) & whole(b - 2), 1, 0)
        before = one + two + three

        def tile(blocks, half):
            row = part * part_size + j * (BLOCK // 2) + half * TILE
            start = (WIN - 1 + j - blocks) * BLOCK
            queries = jnp.concatenate([q_held[part_rows(row, TILE), :], q_mask[part_rows(row, TILE), :]], axis=1)
            edge = blocks * BLOCK + half * (BLOCK // 2)
            pieces = [(at, min(STRETCH, edge - at)) for at in range(0, edge, STRETCH)] + [(edge, BLOCK // 2)]
            peak = None
            for at, size in pieces:
                rows = rows_of(start + at, size)
                keys = jnp.concatenate([kv_held[0, rows, :], k_mask[rows, :]], axis=1)
                s = SCALE * lax.dot_general(
                    queries, keys, (((1,), (1,)), ((), ())), preferred_element_type=jnp.float32
                )
                if at == edge:
                    r = lax.broadcasted_iota(jnp.int32, (TILE, size), 0)
                    place = (r // PART) * TOK_DEV + part * PART + r % PART
                    s = jnp.where(lax.broadcasted_iota(jnp.int32, (TILE, size), 1) <= place, s, -3.0e38)
                scores[half, :, at : at + size] = s
                for g in range(size // 128):
                    group = s[:, g * 128 : (g + 1) * 128]
                    peak = group if peak is None else jnp.maximum(peak, group)
            peak = jnp.broadcast_to(jnp.max(peak, axis=1, keepdims=True), (TILE, 128))
            mixed = totals = None
            for at, size in pieces:
                weights = [jnp.exp2(scores[half, :, at + g * 128 : at + (g + 1) * 128] - peak) for g in range(size // 128)]
                for w in weights:
                    totals = w if totals is None else totals + w
                rounded = jnp.concatenate([w.astype(jnp.bfloat16) for w in weights], axis=1)
                product = jnp.dot(rounded, kv_held[1, rows_of(start + at, size), :], preferred_element_type=jnp.float32)
                mixed = product if mixed is None else mixed + product
            divisor = jnp.broadcast_to(jnp.sum(totals, axis=1, keepdims=True), (TILE, HEAD_WIDTH))
            o_held[part_rows(row, TILE), :] = (mixed / divisor).astype(jnp.bfloat16)

        for blocks in range(WIN):

            @pl.when(before == blocks)
            def _():
                tile(blocks, 0)
                tile(blocks, 1)

        for owner in range(N_HEAD):
            source = o_held.at[part_rows(part * part_size + j * (BLOCK // 2) + owner * PART, PART)]
            goal = out.at[part_rows(part * PART, PART), columns_of(head)]
            mine = (j == x) & (owner == head_index)

            @pl.when(mine)
            def _():
                pltpu.make_async_copy(source, goal, local_sem.at[4 + part]).start()

            @pl.when(jnp.logical_not(mine))
            def _():
                remote(source, goal, out_sem, {"head": owner, "ctx": z * SIDE + j}).start()

        return carry

    lax.fori_loop(0, 2 * SIDE, attend, 0)

    for part in range(2):
        view = o_held.at[pl.ds(0, PART)]
        pltpu.make_async_copy(view, view, local_sem.at[4 + part]).wait()
    wait_rows((2 * SIDE * SIDE - 1) * TOK_DEV, out_sem)
    everything = (2 * 15 + 2 * 16 + 31 + 31) * TOK_DEV
    while_left = everything
    step = SIDE * BLOCK
    while while_left > 0:
        part = min(step, while_left)
        wait_rows(part, send_sem)
        while_left -= part

    def sent_up(slot, carry):
        @pl.when(z + 1 < planes)
        def _():
            @pl.when(reads_halo(z + 1, slot))
            def _():
                wait_rows(SIDE * 2 * TOK_DEV, send_sem)

        @pl.when(reads_halo(z, slot))
        def _():
            wait_rows(SIDE * 2 * TOK_DEV, send_sem)

        return carry

    lax.fori_loop(0, WIN - 1, sent_up, 0)


def per_device(query_matrix, key_matrix, value_matrix, documents, readers):
    tokens = SIDE * BLOCK
    window = SLOTS * BLOCK
    return pl.pallas_call(
        kernel,
        out_shape=jax.ShapeDtypeStruct((TOK_DEV, QUERY_HEADS * HEAD_WIDTH), jnp.bfloat16),
        in_specs=[
            pl.BlockSpec(memory_space=pltpu.SMEM),
            pl.BlockSpec(memory_space=pl.ANY),
            pl.BlockSpec(memory_space=pl.ANY),
            pl.BlockSpec(memory_space=pl.ANY),
            pl.BlockSpec(memory_space=pltpu.VMEM),
        ],
        out_specs=pl.BlockSpec(memory_space=pl.ANY),
        scratch_shapes=[
            pltpu.VMEM((tokens, HEAD_WIDTH), jnp.bfloat16),
            pltpu.VMEM((2, window, HEAD_WIDTH), jnp.bfloat16),
            pltpu.VMEM((tokens, HEAD_WIDTH), jnp.bfloat16),
            pltpu.VMEM((window, HEAD_WIDTH), jnp.bfloat16),
            pltpu.VMEM((2, TILE, WIN * BLOCK), jnp.float32),
            pltpu.VMEM((tokens, HEAD_WIDTH), jnp.bfloat16),
            pltpu.SemaphoreType.DMA((6,)),
            pltpu.SemaphoreType.DMA,
            pltpu.SemaphoreType.DMA((2,)),
            pltpu.SemaphoreType.DMA((SIDE * SIDE,)),
            pltpu.SemaphoreType.DMA,
            pltpu.SemaphoreType.DMA((WIN - 1,)),
            pltpu.SemaphoreType.DMA((WIN - 1,)),
            pltpu.SemaphoreType.DMA,
        ],
        compiler_params=pltpu.CompilerParams(
            collective_id=0, has_side_effects=True, vmem_limit_bytes=60 * 1024 * 1024
        ),
    )(readers.T, query_matrix, key_matrix, value_matrix, documents.reshape(-1, 128))


def solution(mesh):
    placed = (
        P(("ctx", "head"), None),
        P(("ctx", "head"), None),
        P(("ctx", "head"), None),
        P(),
        P(),
    )
    return jax.shard_map(
        per_device, mesh=mesh, in_specs=placed, out_specs=P(("ctx", "head"), None), check_vma=False
    )
```

time: 74.1 us -> 57.9 us (0.78); the launches traced: 74 us -> 56.8 us
  Pallas kernels: 71.7 us -> 54.5 us
    pallas_call x1, Pallas kernels: 71.7 us -> 54.5 us  [per_device(): pl.pallas_call(kernel, out_shape=jax.ShapeDtypeStruct((TOK_DEV, QUERY_HEA...]
where the time goes in v2:
time: 57.9 us; the launch traced here: 56.8 us
  Pallas kernels  54.5 us (94%)
  local copies, waits for them, and re-layouts  2.29 us (4%)
    pallas_call x1, Pallas kernels, per_device(): pl.pallas_call(kernel, out_shape=jax.ShapeDtypeStruct((TOK_DEV, QUERY_HEA...  54.5 us
    unnamed x1, local copies, waits for them, and re-layouts  2.29 us

profile of v2, /device:TPU:153, one launch (start us, length us, event | category | flops | bytes accessed | tf_op | source)
XLA Modules:
  0.0 56.8 jit_solution(9831617682181847274)
XLA Ops:
  0.0 54.5 %shard_map.55 = bf16[128,4096]{1,0:T(8,128)(2,1)} custom-call(s32[4,32]{1,0:T(4,128)} %bitcast.3, bf16[128,4096]{1,0:T(8,128)(2,1)} %q_in.1, bf16[128,2048]{1,0:T(8,128)(2,1)} %k_in.1, bf16[128,2048]{1,0:T(8,128)(2,1)} %v_in.1, s32[256,128]{1,0:T(8,128)} %bitcast.2), custom_call_target="tpu_custom_call" | custom-call | tf_op jit(solution)/shard_map/pallas_call | solution.py:373
  54.5 2.3 %copy.7 = bf16[128,4096]{1,0:T(8,128)(2,1)} copy(bf16[128,4096]{1,0:T(8,128)(2,1)} %shard_map.55) | data formatting | bytes 2097152

commit v3 on v2

--- a/solution.py
+++ b/solution.py
@@ -15,9 +15,9 @@
 SIDE = 4
 SLOTS = SIDE + WIN - 1
 PART = TOK_DEV // 2
-TILE = 256
+TILE = 512
 STRETCH = 1024
-EARLY = 20
+EARLY = 32
 
 SCALE = 168.0**-0.5 * 1.4426950408889634
 STEP = 16384.0
@@ -175,6 +175,12 @@
         ).start()
 
 
+    def send_first(i, carry):
+        send_q(i, 0)
+        return carry
+
+    lax.fori_loop(1, 2 * SIDE * SIDE, send_first, 0)
+
     def pass_on(i, carry):
         dx, dy = offset(i)
         X, Y, C = device(SIDE - dx, SIDE - dy, 0)
@@ -212,16 +218,6 @@
             def _():
                 to_next_plane(X, Y)
 
-        @pl.when(i > 0)
-        def _():
-            send_q(2 * i, 0)
-
-        send_q(2 * i + 1, 0)
-
-        @pl.when(EARLY + i < SIDE * groups)
-        def _():
-            own_mask(EARLY + i, 0)
-
         @pl.when((i >= groups) & reads_halo(z, WIN - 2))
         def _():
             key_mask(WIN - 2, i - groups)
@@ -282,45 +278,54 @@
         three = jnp.where((b >= 3) & whole(b - 1) & whole(b - 2), 1, 0)
         before = one + two + three
 
-        def tile(blocks, half):
-            row = part * part_size + j * (BLOCK // 2) + half * TILE
+        def tile(blocks):
+            row = part * part_size + j * TILE
             start = (WIN - 1 + j - blocks) * BLOCK
+            edge = blocks * BLOCK
+            late = TILE // 2
             queries = jnp.concatenate([q_held[part_rows(row, TILE), :], q_mask[part_rows(row, TILE), :]], axis=1)
-            edge = blocks * BLOCK + half * (BLOCK // 2)
-            pieces = [(at, min(STRETCH, edge - at)) for at in range(0, edge, STRETCH)] + [(edge, BLOCK // 2)]
-            peak = None
-            for at, size in pieces:
+            pieces = [(at, STRETCH, 0) for at in range(0, edge, STRETCH)]
+            pieces += [(edge, BLOCK // 2, 0), (edge + BLOCK // 2, BLOCK // 2, late)]
+            peak = [None, None]
+
+            def merged(old, new, first, join):
+                halves = [new[:, :late], new[:, late:]] if first == 0 else [None, new]
+                return [o if n is None else n if o is None else join(o, n) for o, n in zip(old, halves)]
+
+            for at, size, first in pieces:
                 rows = rows_of(start + at, size)
                 keys = jnp.concatenate([kv_held[0, rows, :], k_mask[rows, :]], axis=1)
                 s = SCALE * lax.dot_general(
-                    queries, keys, (((1,), (1,)), ((), ())), preferred_element_type=jnp.float32
+                    keys, queries[first:], (((1,), (1,)), ((), ())), preferred_element_type=jnp.float32
                 )
-                if at == edge:
-                    r = lax.broadcasted_iota(jnp.int32, (TILE, size), 0)
+                if at >= edge:
+                    r = lax.broadcasted_iota(jnp.int32, s.shape, 1) + first
                     place = (r // PART) * TOK_DEV + part * PART + r % PART
-                    s = jnp.where(lax.broadcasted_iota(jnp.int32, (TILE, size), 1) <= place, s, -3.0e38)
-                scores[half, :, at : at + size] = s
-                for g in range(size // 128):
-                    group = s[:, g * 128 : (g + 1) * 128]
-                    peak = group if peak is None else jnp.maximum(peak, group)
-            peak = jnp.broadcast_to(jnp.max(peak, axis=1, keepdims=True), (TILE, 128))
-            mixed = totals = None
-            for at, size in pieces:
-                weights = [jnp.exp2(scores[half, :, at + g * 128 : at + (g + 1) * 128] - peak) for g in range(size // 128)]
-                for w in weights:
-                    totals = w if totals is None else totals + w
-                rounded = jnp.concatenate([w.astype(jnp.bfloat16) for w in weights], axis=1)
-                product = jnp.dot(rounded, kv_held[1, rows_of(start + at, size), :], preferred_element_type=jnp.float32)
-                mixed = product if mixed is None else mixed + product
-            divisor = jnp.broadcast_to(jnp.sum(totals, axis=1, keepdims=True), (TILE, HEAD_WIDTH))
-            o_held[part_rows(row, TILE), :] = (mixed / divisor).astype(jnp.bfloat16)
+                    s = jnp.where(lax.broadcasted_iota(jnp.int32, s.shape, 0) + (at - edge) <= place, s, -3.0e38)
+                scores[at : at + size, first:] = s
+                peak = merged(peak, jnp.max(s, axis=0, keepdims=True), first, jnp.maximum)
+            mixed = [None, None]
+            totals = [None, None]
+            for at, size, first in pieces:
+                top = peak[1] if first else jnp.concatenate(peak, axis=1)
+                weights = jnp.exp2(scores[at : at + size, first:] - top)
+                totals = merged(totals, jnp.sum(weights, axis=0, keepdims=True), first, jnp.add)
+                product = lax.dot_general(
+                    kv_held[1, rows_of(start + at, size), :],
+                    weights.astype(jnp.bfloat16),
+                    (((0,), (0,)), ((), ())),
+                    preferred_element_type=jnp.float32,
+                )
+                mixed = merged(mixed, product, first, jnp.add)
+            for n in range(2):
+                answers = jnp.transpose(mixed[n] / totals[n]).astype(jnp.bfloat16)
+                o_held[part_rows(row + n * late, late), :] = answers
 
         for blocks in range(WIN):
 
             @pl.when(before == blocks)
             def _():
-                tile(blocks, 0)
-                tile(blocks, 1)
+                tile(blocks)
 
         for owner in range(N_HEAD):
             source = o_held.at[part_rows(part * part_size + j * (BLOCK // 2) + owner * PART, PART)]
@@ -386,7 +391,7 @@
             pltpu.VMEM((2, window, HEAD_WIDTH), jnp.bfloat16),
             pltpu.VMEM((tokens, HEAD_WIDTH), jnp.bfloat16),
             pltpu.VMEM((window, HEAD_WIDTH), jnp.bfloat16),
-            pltpu.VMEM((2, TILE, WIN * BLOCK), jnp.float32),
+            pltpu.VMEM((WIN * BLOCK, TILE), jnp.float32),
             pltpu.VMEM((tokens, HEAD_WIDTH), jnp.bfloat16),
             pltpu.SemaphoreType.DMA((6,)),
             pltpu.SemaphoreType.DMA,

time: 57.9 us -> 55.1 us (0.952)
  Pallas kernels: 54.5 us -> 52.1 us
    pallas_call x1, Pallas kernels: 54.5 us -> 52.1 us  [per_device(): pl.pallas_call(kernel, out_shape=jax.ShapeDtypeStruct((TOK_DEV, QUERY_HEA...]
where the time goes in v3:
time: 55.1 us; the launch traced here: 54.4 us
  Pallas kernels  52.1 us (95%)
  local copies, waits for them, and re-layouts  2.29 us (4%)
    pallas_call x1, Pallas kernels, per_device(): pl.pallas_call(kernel, out_shape=jax.ShapeDtypeStruct((TOK_DEV, QUERY_HEA...  52.1 us
    unnamed x1, local copies, waits for them, and re-layouts  2.29 us

profile of v3, /device:TPU:153, one launch (start us, length us, event | category | flops | bytes accessed | tf_op | source)
XLA Modules:
  0.0 54.4 jit_solution(1178482132517828058)
XLA Ops:
  0.0 52.1 %shard_map.55 = bf16[128,4096]{1,0:T(8,128)(2,1)} custom-call(s32[4,32]{1,0:T(4,128)} %bitcast.3, bf16[128,4096]{1,0:T(8,128)(2,1)} %q_in.1, bf16[128,2048]{1,0:T(8,128)(2,1)} %k_in.1, bf16[128,2048]{1,0:T(8,128)(2,1)} %v_in.1, s32[256,128]{1,0:T(8,128)} %bitcast.2), custom_call_target="tpu_custom_call" | custom-call | tf_op jit(solution)/shard_map/pallas_call | solution.py:378
  52.1 2.3 %copy.7 = bf16[128,4096]{1,0:T(8,128)(2,1)} copy(bf16[128,4096]{1,0:T(8,128)(2,1)} %shard_map.55) | data formatting | bytes 2097152

commit v4 on v3

--- a/solution.py
+++ b/solution.py
@@ -39,9 +39,9 @@
 
 
 def kernel(
-    readers, q_in, k_in, v_in, documents,
+    readers_in, q_in, k_in, v_in, documents_in,
     out,
-    q_held, kv_held, q_mask, k_mask, scores, o_held,
+    readers, documents, q_held, kv_held, q_mask, k_mask, scores, o_held,
     local_sem, send_sem, q_sem, kv_sem, twin_sem, halo_sem, halo_twin_sem, out_sem,
 ):
     head_index = lax.axis_index("head")
@@ -58,6 +58,13 @@
 
     def target(X, Y, C):
         return {"head": Y * 2 + C, "ctx": z * SIDE + X}
+
+    small_copies = [
+        pltpu.make_async_copy(readers_in, readers, local_sem.at[6]),
+        pltpu.make_async_copy(documents_in, documents, local_sem.at[7]),
+    ]
+    for copy in small_copies:
+        copy.start()
 
     barrier = pltpu.get_barrier_semaphore()
 
@@ -111,6 +118,8 @@
             q_mask[part_rows(part * (SIDE * BLOCK // 2) + n * PART, PART), :] = wanted[part * PART : (part + 1) * PART]
         return carry
 
+    for copy in small_copies:
+        copy.wait()
     lax.fori_loop(0, EARLY, own_mask, 0)
 
     neighbours = jnp.where(z > 0, 1, 0) + jnp.where(z + 1 < planes, 1, 0)
@@ -247,7 +256,6 @@
 
         return carry
 
-    lax.fori_loop(0, WIN - 1, take_halo, 0)
     wait_rows(SIDE * SIDE * 2 * TOK_DEV, twin_sem)
 
     def halo_here(slot, carry):
@@ -257,13 +265,28 @@
 
         return carry
 
-    lax.fori_loop(0, WIN - 1, halo_here, 0)
 
     head = chip * 2 + core
+
+    far = reads_halo(z, 0)
+    needing = jnp.where(whole(own_block), 2, 1)
+    use_at = jnp.where(far, SIDE - needing, 0)
+    take_at = jnp.where(far, 1, 0)
 
     def attend(t, carry):
         part = t // SIDE
-        j = (x + 1 + t % SIDE) % SIDE
+        turn = (x + 1 + t % SIDE) % SIDE
+        one_last = jnp.where(t < SIDE - 1, 1 + (x + t) % (SIDE - 1), 0)
+        two_last = jnp.where(t < SIDE - 2, 2, 0) + (x + t) % 2
+        j = jnp.where(far & (part == 0), jnp.where(needing == 1, one_last, two_last), turn)
+
+        @pl.when(t == take_at)
+        def _():
+            lax.fori_loop(0, WIN - 1, take_halo, 0)
+
+        @pl.when(t == use_at)
+        def _():
+            lax.fori_loop(0, WIN - 1, halo_here, 0)
 
         @pl.when(t % SIDE == 0)
         def _():
@@ -379,21 +402,23 @@
         kernel,
         out_shape=jax.ShapeDtypeStruct((TOK_DEV, QUERY_HEADS * HEAD_WIDTH), jnp.bfloat16),
         in_specs=[
-            pl.BlockSpec(memory_space=pltpu.SMEM),
             pl.BlockSpec(memory_space=pl.ANY),
             pl.BlockSpec(memory_space=pl.ANY),
             pl.BlockSpec(memory_space=pl.ANY),
-            pl.BlockSpec(memory_space=pltpu.VMEM),
+            pl.BlockSpec(memory_space=pl.ANY),
+            pl.BlockSpec(memory_space=pl.ANY),
         ],
         out_specs=pl.BlockSpec(memory_space=pl.ANY),
         scratch_shapes=[
+            pltpu.SMEM(readers.shape[::-1], jnp.int32),
+            pltpu.VMEM((documents.shape[0] // TOK_DEV, TOK_DEV), jnp.int32),
             pltpu.VMEM((tokens, HEAD_WIDTH), jnp.bfloat16),
             pltpu.VMEM((2, window, HEAD_WIDTH), jnp.bfloat16),
             pltpu.VMEM((tokens, HEAD_WIDTH), jnp.bfloat16),
             pltpu.VMEM((window, HEAD_WIDTH), jnp.bfloat16),
             pltpu.VMEM((WIN * BLOCK, TILE), jnp.float32),
             pltpu.VMEM((tokens, HEAD_WIDTH), jnp.bfloat16),
-            pltpu.SemaphoreType.DMA((6,)),
+            pltpu.SemaphoreType.DMA((8,)),
             pltpu.SemaphoreType.DMA,
             pltpu.SemaphoreType.DMA((2,)),
             pltpu.SemaphoreType.DMA((SIDE * SIDE,)),

time: 55.1 us -> 54.3 us (0.985)
  Pallas kernels: 52.1 us -> 51 us
    pallas_call x1, Pallas kernels: 52.1 us -> 51 us  [per_device(): pl.pallas_call(kernel, out_shape=jax.ShapeDtypeStruct((TOK_DEV, QUERY_HEA...]
where the time goes in v4:
time: 54.3 us; the launch traced here: 53.3 us
  Pallas kernels  51 us (94%)
  local copies, waits for them, and re-layouts  2.29 us (4%)
    pallas_call x1, Pallas kernels, per_device(): pl.pallas_call(kernel, out_shape=jax.ShapeDtypeStruct((TOK_DEV, QUERY_HEA...  51 us
    unnamed x1, local copies, waits for them, and re-layouts  2.29 us

profile of v4, /device:TPU:153, one launch (start us, length us, event | category | flops | bytes accessed | tf_op | source)
XLA Modules:
  0.0 53.3 jit_solution(866002247408449495)
XLA Ops:
  0.0 51.0 %shard_map.55 = bf16[128,4096]{1,0:T(8,128)(2,1)} custom-call(s32[4,32]{1,0:T(4,128)} %bitcast.3, bf16[128,4096]{1,0:T(8,128)(2,1)} %q_in.1, bf16[128,2048]{1,0:T(8,128)(2,1)} %k_in.1, bf16[128,2048]{1,0:T(8,128)(2,1)} %v_in.1, s32[256,128]{1,0:T(8,128)} %bitcast.2), custom_call_target="tpu_custom_call" | custom-call | tf_op jit(solution)/shard_map/pallas_call | solution.py:401
  51.0 2.3 %copy.7 = bf16[128,4096]{1,0:T(8,128)(2,1)} copy(bf16[128,4096]{1,0:T(8,128)(2,1)} %shard_map.55) | data formatting | bytes 2097152
